TPU v7x, 32 devices: a whole 2x2x4 slice. The times are simulated.
32 devices in a mesh: grp: 16 (over z, x, core), slab: 2 (over y).
Axes of the slice: x: 2, y: 2, z: 4, core: 2. Of those that a mesh axis runs over, the one named last changes fastest.
Arguments:
- ligand_grids: float32 [2, 4, 128, 128, 128], P(None, None, 'grp', 'slab'), may hold values from -6 to 6
- receptor_kernel: bfloat16 [16, 2, 2, 128, 128, 128], P('grp', None, None, 'slab'), may hold values from -3 to 3
Outputs:
- best_score: bfloat16 [16, 128, 128, 128], P('grp', None, 'slab')
All inputs are finite; a program needn't handle non-finite values.
Results may differ from a plain program's by a relative error of at most 0.018.
Values may be sent and summed in bfloat16 or wider, within the bound.
A program may use at most 128 MiB of HBM per device.

v0:
```python
import math
import jax
import jax.numpy as jnp
from jax import lax
from jax.sharding import PartitionSpec as P

highest = lax.Precision.HIGHEST


def coefficients(length, inverse):
    positions = jnp.arange(length, dtype=jnp.int32)
    phases = positions[:, None] * positions[None, :] % length
    angles = phases.astype(jnp.float32) * (2.0 * math.pi / length)
    scaling = 1.0 / math.sqrt(length)
    cosine = jnp.cos(angles) * scaling
    sine_part = jnp.sin(angles) * scaling
    if inverse:
        sine_part = -sine_part
    upper_rows = jnp.stack([cosine, sine_part])
    lower_rows = jnp.stack([-sine_part, cosine])
    return jnp.stack([upper_rows, lower_rows])


def pack_pairs(ligand_piece):
    stacked = jnp.stack([ligand_piece[:, 0::2], ligand_piece[:, 1::2]])
    return stacked.reshape((2, stacked.shape[1] * stacked.shape[2]) + stacked.shape[3:])


def body(ligand_grids, receptor_kernel):
    length = ligand_grids.shape[4]
    rotations = ligand_grids.shape[0]
    channel_pairs = ligand_grids.shape[1] // 2
    forward = coefficients(length, False)
    forward_low = forward.astype(jnp.bfloat16)
    inverse_low = coefficients(length, True).astype(jnp.bfloat16)
    packed = pack_pairs(ligand_grids)
    lines = jnp.einsum("pqkn,qrzxn->pkrzx", forward, packed, precision=highest)
    columns = lax.all_to_all(
        lines.astype(jnp.bfloat16), "grp", split_axis=1, concat_axis=3, tiled=True
    ).astype(lines.dtype)
    partial_value = jnp.einsum("pqkn,qyrnx->pyrkx", forward, columns, precision=highest).astype(
        jnp.bfloat16
    )
    pieces = jnp.einsum(
        "pqkn,qyrzn->pyrzk",
        forward_low,
        lax.all_to_all(partial_value, "slab", split_axis=3, concat_axis=4, tiled=True),
        preferred_element_type=jnp.float32,
    ).astype(jnp.bfloat16)
    collected = lax.all_gather(pieces, "grp", axis=1, tiled=True)
    spectrum = jnp.transpose(collected, (0, 2, 3, 4, 1))
    spec_split = spectrum.reshape((2, rotations, channel_pairs) + spectrum.shape[2:])
    kernel_one = receptor_kernel[0]
    kernel_real = kernel_one[0][None].astype(jnp.float32)
    kernel_imag = kernel_one[1][None].astype(jnp.float32)
    spec_real = spec_split[0].astype(jnp.float32)
    spec_imag = spec_split[1].astype(jnp.float32)
    real_part = jnp.sum(kernel_real * spec_real - kernel_imag * spec_imag, axis=1)
    imag_part = jnp.sum(kernel_real * spec_imag + kernel_imag * spec_real, axis=1)
    product = jnp.stack([real_part, imag_part]).astype(jnp.bfloat16)
    rows_done = jnp.einsum(
        "pqkn,qrznm->przkm", inverse_low, product, preferred_element_type=jnp.float32
    ).astype(jnp.bfloat16)
    planes = jnp.einsum(
        "pqkn,qrzxn->przxk", inverse_low, rows_done, preferred_element_type=jnp.float32
    ).astype(jnp.bfloat16)
    scores = jnp.einsum(
        "qkn,qrnxy->rkxy",
        inverse_low[0],
        lax.all_to_all(planes, "slab", split_axis=3, concat_axis=2, tiled=True),
        preferred_element_type=jnp.float32,
    )
    return jnp.max(scores, axis=0).astype(jnp.bfloat16)[None]


def solution(mesh):
    return jax.shard_map(
        body,
        mesh=mesh,
        in_specs=(P(None, None, "grp", "slab", None), P("grp", None, None, "slab", None, None)),
        out_specs=P("grp", None, "slab", None),
        check_vma=False,
    )
```

profile of v0, /device:TPU:0, one launch (start us, length us, event | category | flops | bytes accessed | tf_op | source)
XLA Modules:
  0.0 428.6 jit_solution(18179298888462412341)
XLA Ops:
  6.5 0.3 sine_multiply_fusion
  7.1 1.7 fusion.59
  8.8 1.8 bitcast_convert_fusion.6
  10.6 3.0 copy.32
  13.6 1.5 reshape.162
  15.1 31.9 %all_to_all.54 = bf16[16,2,16384]{2,1,0:T(2,128)(2,1)S(1)} all-to-all(bf16[16,2,16384]{2,1,0:T(2,128)(2,1)S(1)} %reshape.162), channel_id=1, replica_groups=mesh['grp'=16,'slab'=2] {'grp'}, dimensions={0} | all-to-all | bytes 2097152 | tf_op jit(solution)/shard_map/all_to_all | solution.py:38
  47.0 1.3 reshape.163
  48.3 3.0 fusion.26
  51.3 4.8 %copy.36 = bf16[2,8,4,128,64]{4,0,2,1,3:T(2,128)(2,1)S(1)} copy(bf16[2,8,4,128,64]{3,4,0,2,1:T(8,128)(2,1)} %fusion.26) | data formatting | bytes 2097152 | tf_op jit(solution)/shard_map/convert_element_type | solution.py:41
  56.1 1.6 reshape.164
  57.8 18.4 %all_to_all.55 = bf16[2,2,131072]{2,1,0:T(2,128)(2,1)} all-to-all(bf16[2,2,131072]{2,1,0:T(2,128)(2,1)S(1)} %reshape.164), channel_id=1, replica_groups=mesh['grp'=16,'slab'=2] {'slab'}, dimensions={0} | all-to-all | bytes 2097152 | tf_op jit(solution)/shard_map/all_to_all | solution.py:47
  76.2 2.6 reshape.165
  78.8 3.5 copy.90
  82.3 3.9 reshape.151
  86.2 0.5 fusion.29
  86.7 1.1 copy.38
  87.8 11.8 %bitcast_convert_fusion.3 = (f32[2,64,128,128]{3,2,1,0:T(8,128)}, f32[2,64,128,128]{3,2,1,0:T(8,128)}) fusion(bf16[1,2,2,64,128,128]{5,4,3,2,1,0:T(8,128)(2,1)} %param.3), kind=kLoop, calls=%fused_computation.25 | loop fusion | flops 4194304 | bytes 25165824 | tf_op jit(solution)/shard_map/convert_element_type | solution.py:54
  99.5 8.7 %copy.31 = f32[2,64,128,128]{2,1,0,3:T(8,128)} copy(f32[2,64,128,128]{3,2,1,0:T(8,128)} %get-tuple-element.9) | data formatting | bytes 16777216 | tf_op jit(solution)/shard_map/convert_element_type | solution.py:54
  108.3 8.8 %copy.39 = f32[2,64,128,128]{2,1,0,3:T(8,128)} copy(f32[2,64,128,128]{3,2,1,0:T(8,128)} %get-tuple-element.10) | data formatting | bytes 16777216 | tf_op jit(solution)/shard_map/convert_element_type | solution.py:55
  117.3 0.3 fusion.48
  117.6 95.5 %all-gather.2.cloned.1.call-done = bf16[2,128,4,64,128]{4,3,2,0,1:T(8,128)(2,1)} async-done(((bf16[2,8,4,64,128]{4,3,2,0,1:T(8,128)(2,1)}), bf16[2,128,4,64,128]{4,3,2,0,1:T(8,128)(2,1)}) %all-gather.2.cloned.1.call-update) | async-done | bytes 16777232 | tf_op jit(solution)/shard_map/all_gather | solution.py:50
  213.2 15.2 %fusion.58 = (bf16[1,4,64,128,128]{3,2,1,0,4:T(8,128)(2,1)}, bf16[1,4,64,128,128]{3,2,1,0,4:T(8,128)(2,1)}) fusion(bf16[2,4,64,128,128]{3,2,1,0,4:T(8,128)(2,1)} %bitcast.146), kind=kLoop, calls=%fused_computation.75 | loop fusion | bytes 33554432 | tf_op jit(solution)/shard_map/slice | solution.py:56
  228.4 17.3 %fusion.1 = (bf16[2,64,128,128]{2,1,0,3:T(8,128)(2,1)}, bf16[2,64,128,128]{2,1,0,3:T(8,128)(2,1)}) fusion(bf16[2,2,64,128,128]{3,2,1,0,4:T(8,128)(2,1)} %bitcast.144, bf16[2,2,64,128,128]{3,2,1,0,4:T(8,128)(2,1)} %bitcast.143, f32[2,64,128,128]{2,1,0,3:T(8,128)} %copy.39, f32[2,64,128,128]{2,1,0,3:T(8,128)S(1)} %copy-done), kind=kLoop, calls=%fused_computation.5 | loop fusion | flops 37748736 | bytes 41943040 | tf_op jit(solution)/shard_map/reduce_sum | solution.py:58
  245.7 7.0 %copy.88 = bf16[2,64,128,128]{2,3,1,0:T(8,128)(2,1)} copy(bf16[2,64,128,128]{2,1,0,3:T(8,128)(2,1)} %get-tuple-element.5) | data formatting | bytes 8388608 | tf_op jit(solution)/shard_map/reduce_sum | solution.py:58
  252.6 4.6 %copy.89 = bf16[2,64,128,128]{2,3,1,0:T(8,128)(2,1)} copy(bf16[2,64,128,128]{2,1,0,3:T(8,128)(2,1)S(1)} %copy-done.1) | data formatting | bytes 8388608 | tf_op jit(solution)/shard_map/reduce_sum | solution.py:59
  257.3 9.3 %fusion.7 = bf16[2,2,64,128,128]{4,3,0,2,1:T(8,128)(2,1)} fusion(bf16[1,2,64,128,128]{3,4,0,2,1:T(8,128)(2,1)} %bitcast.153, bf16[1,2,64,128,128]{3,4,0,2,1:T(8,128)(2,1)} %bitcast.152, bf16[1,2,128,128]{3,2,1,0:T(8,128)(2,1)S(1)} %get-tuple-element.16, bf16[1,2,128,128]{3,2,1,0:T(8,128)(2,1)S(1)} %get-tuple-element.15), kind=kOutput, calls=%fused_computation.12 | convolution fusion | flops 4320657408 | bytes 16908288 | tf_op jit(solution)/shard_map/pqkn,qrzxn->przxk/dot_general | solution.py:64
  266.6 12.2 %copy.43 = bf16[2,2,64,128,128]{4,0,2,1,3:T(2,128)(2,1)S(1)} copy(bf16[2,2,64,128,128]{4,3,0,2,1:T(8,128)(2,1)} %fusion.7) | data formatting | bytes 16777216 | tf_op jit(solution)/shard_map/convert_element_type | solution.py:66
  278.8 97.3 %all_to_all.56 = bf16[2,2,64,128,128]{4,0,2,1,3:T(2,128)(2,1)} all-to-all(bf16[2,2,64,128,128]{4,0,2,1,3:T(2,128)(2,1)S(1)} %copy.43), channel_id=1, replica_groups=mesh['grp'=16,'slab'=2] {'slab'}, dimensions={3} | all-to-all | bytes 16777216 | tf_op jit(solution)/shard_map/all_to_all | solution.py:70
  376.1 12.0 %copy.44 = bf16[2,2,64,128,128]{4,3,2,1,0:T(8,128)(2,1)} copy(bf16[2,2,64,128,128]{4,0,2,1,3:T(2,128)(2,1)} %all_to_all.56) | data formatting | bytes 16777216 | tf_op jit(solution)/shard_map/all_to_all | solution.py:70
  388.1 9.4 %copy.45 = bf16[2,2,2,64,64,128]{5,4,3,2,1,0:T(8,128)(2,1)} copy(bf16[2,2,2,64,64,128]{5,4,2,3,1,0:T(8,128)(2,1)} %bitcast.145) | data formatting | bytes 16777216 | tf_op jit(solution)/shard_map/all_to_all | solution.py:70
  397.5 21.2 %bitcast_reduce_fusion = bf16[64,128,128]{2,1,0:T(8,128)(2,1)S(1)} fusion(bf16[2,2,128,64,128]{4,3,2,1,0:T(8,128)(2,1)} %bitcast.149, bf16[1,128,128]{2,1,0:T(8,128)(2,1)S(1)} %get-tuple-element.20, bf16[1,128,128]{2,1,0:T(8,128)(2,1)S(1)} %fusion.51), kind=kOutput, calls=%fused_computation.17 | convolution fusion | flops 1074823168 | bytes 10551296 | tf_op jit(solution)/shard_map/qkn,qrnxy->rkxy/dot_general | solution.py:67
  418.7 2.8 copy.47
  (10 shorter events, 0.6 us)
Async XLA Ops:
  6.5 206.6 %all-gather.2.cloned.1.call-start = ((), (), s32[]{:S(2)}) async-start(), calls=%async_computation.3 | async-start | bytes 17825792 | tf_op jit(solution)/shard_map/all_gather | solution.py:50
  213.2 15.2 %copy-start = (f32[2,64,128,128]{2,1,0,3:T(8,128)S(1)}, f32[2,64,128,128]{2,1,0,3:T(8,128)}, u32[]{:S(2)}) copy-start(f32[2,64,128,128]{2,1,0,3:T(8,128)} %copy.31) | copy-start | bytes 25165828
  245.7 7.0 %copy-start.1 = (bf16[2,64,128,128]{2,1,0,3:T(8,128)(2,1)S(1)}, bf16[2,64,128,128]{2,1,0,3:T(8,128)(2,1)}, u32[]{:S(2)}) copy-start(bf16[2,64,128,128]{2,1,0,3:T(8,128)(2,1)} %get-tuple-element.6) | copy-start | bytes 12582916
Sparse Core Ops, SparseCore 0:
  87.9 125.2 all-gather.1
where the time goes:
time: 436 us; the launch traced here: 429 us
  blocking collectives  148 us (34%)
  local copies, waits for them, and re-layouts  106 us (24%)
  waiting for transfers between devices  95.6 us (22%)
  matrix products  35.9 us (8%)
  other arithmetic  30.2 us (7%)
  between operations  13.7 us (3%)
    all_to_all x1, blocking collectives, body(): lax.all_to_all(planes, 'slab', split_axis=3, concat_axis=2, tiled=True)  97.3 us
    all_gather x1, waiting for transfers between devices, body(): collected = lax.all_gather(pieces, 'grp', axis=1, tiled=True)  95.5 us
    all_to_all x1, blocking collectives, body(): lax.all_to_all(lines.astype(jnp.bfloat16), 'grp', split_axis=1, concat_ax...  31.9 us
    all_to_all x2, local copies, waits for them, and re-layouts, body(): lax.all_to_all(planes, 'slab', split_axis=3, concat_axis=2, tiled=True)  21.4 us
    dot_general x1, matrix products, body(): jnp.einsum('qkn,qrnxy->rkxy', inverse_low[0], lax.all_to_all(planes, 'sla...  21.2 us
    all_to_all x1, blocking collectives, body(): lax.all_to_all(partial_value, 'slab', split_axis=3, concat_axis=4, tiled=...  18.4 us
    reduce_sum x1, other arithmetic, body(): jnp.sum(kernel_real * spec_real - kernel_imag * spec_imag, axis=1)  17.3 us
    slice x1, local copies, waits for them, and re-layouts, body(): spec_real = spec_split[0].astype(jnp.float32)  15.2 us
  transfers between devices with their start and end apart: 1, of which 1 were waited for; matrix products, arithmetic and copies ran while one was open for 7% of the time, Pallas kernels for 0%

commit v1 on v0

--- a/solution.py
+++ b/solution.py
@@ -27,6 +27,18 @@
 
 
 def body(ligand_grids, receptor_kernel):
+
+    def read_edge(x_local):
+        return jnp.concatenate(
+            jax.lax.all_to_all(
+                jnp.stack(jnp.split(x_local, jax.lax.psum(1, axis_name="slab"), axis=3), axis=0),
+                split_axis=0,
+                axis_name="slab",
+                concat_axis=0,
+            ),
+            axis=4,
+        )
+
     length = ligand_grids.shape[4]
     rotations = ligand_grids.shape[0]
     channel_pairs = ligand_grids.shape[1] // 2
@@ -44,7 +56,7 @@
     pieces = jnp.einsum(
         "pqkn,qyrzn->pyrzk",
         forward_low,
-        lax.all_to_all(partial_value, "slab", split_axis=3, concat_axis=4, tiled=True),
+        read_edge(partial_value),
         preferred_element_type=jnp.float32,
     ).astype(jnp.bfloat16)
     collected = lax.all_gather(pieces, "grp", axis=1, tiled=True)

time: 436 us -> 432 us (level)
  local copies, waits for them, and re-layouts: 106 us -> 101 us
    all_to_all x2 -> x0, local copies, waits for them, and re-layouts: 7.4 us -> none  [body(): lax.all_to_all(partial_value, 'slab', split_axis=3, concat_axis=4, tiled=...]
    reshape x0 -> x3, local copies, waits for them, and re-layouts: none -> 7.26 us  [read_edge(): jnp.concatenate(jax.lax.all_to_all(jnp.stack(jnp.split(x_local, jax.lax.p...]
    convert_element_type x2 -> x1, local copies, waits for them, and re-layouts: 5.88 us -> 1.06 us  [body(): pieces = jnp.einsum('pqkn,qyrzn->pyrzk', forward_low, read_edge(partial_v...]
where the time goes in v1:
time: 432 us; the launch traced here: 424 us
  blocking collectives  148 us (34%)
  local copies, waits for them, and re-layouts  101 us (23%)
  waiting for transfers between devices  95.5 us (22%)
  matrix products  35 us (8%)
  other arithmetic  30.8 us (7%)
  between operations  14 us (3%)
    all_to_all x1, blocking collectives, body(): lax.all_to_all(planes, 'slab', split_axis=3, concat_axis=2, tiled=True)  97.3 us
    all_gather x1, waiting for transfers between devices, body(): collected = lax.all_gather(pieces, 'grp', axis=1, tiled=True)  95.5 us
    all_to_all x1, blocking collectives, body(): lax.all_to_all(lines.astype(jnp.bfloat16), 'grp', split_axis=1, concat_ax...  31.9 us
    all_to_all x2, local copies, waits for them, and re-layouts, body(): lax.all_to_all(planes, 'slab', split_axis=3, concat_axis=2, tiled=True)  21.4 us
    dot_general x1, matrix products, body(): jnp.einsum('qkn,qrnxy->rkxy', inverse_low[0], lax.all_to_all(planes, 'sla...  21.3 us
    all_to_all x1, blocking collectives, read_edge(): jax.lax.all_to_all(jnp.stack(jnp.split(x_local, jax.lax.psum(1, axis_name...  18.4 us
    reduce_sum x1, other arithmetic, body(): jnp.sum(kernel_real * spec_real - kernel_imag * spec_imag, axis=1)  17.5 us
    slice x1, local copies, waits for them, and re-layouts, body(): spec_real = spec_split[0].astype(jnp.float32)  15.2 us
  transfers between devices with their start and end apart: 1, of which 1 were waited for; matrix products, arithmetic and copies ran while one was open for 7% of the time, Pallas kernels for 0%

profile of v1, /device:TPU:0, one launch (start us, length us, event | category | flops | bytes accessed | tf_op | source)
XLA Modules:
  0.0 424.2 jit_solution(11594017238358159139)
XLA Ops:
  7.1 1.7 fusion.59
  8.8 1.8 bitcast_convert_fusion.6
  10.6 3.0 copy.32
  13.6 1.5 reshape.171
  15.1 31.9 %all_to_all.41 = bf16[16,2,16384]{2,1,0:T(2,128)(2,1)S(1)} all-to-all(bf16[16,2,16384]{2,1,0:T(2,128)(2,1)S(1)} %reshape.171), channel_id=1, replica_groups=mesh['grp'=16,'slab'=2] {'grp'}, dimensions={0} | all-to-all | bytes 2097152 | tf_op jit(solution)/shard_map/all_to_all | solution.py:50
  47.0 1.3 reshape.172
  48.3 2.0 fusion.26
  50.4 0.5 slice_bitcast_fusion.1
  50.9 0.5 fusion.60
  51.3 1.6 reshape.173
  53.0 18.4 %all_to_all.42 = bf16[2,2,131072]{2,1,0:T(2,128)(2,1)} all-to-all(bf16[2,2,131072]{2,1,0:T(2,128)(2,1)S(1)} %reshape.173), channel_id=1, replica_groups=mesh['grp'=16,'slab'=2] {'slab'}, dimensions={0} | all-to-all | bytes 2097152 | tf_op jit(solution)/shard_map/all_to_all | solution.py:33
  71.4 2.6 reshape.174
  74.0 1.5 bitcast_bitcast_fusion
  75.5 4.8 %copy.66 = bf16[2,8,4,64,2,64]{5,4,3,0,2,1:T(2,128)(2,1)S(1)} copy(bf16[2,8,4,64,2,64]{3,5,0,2,1,4:T(8,128)(2,1)} %bitcast_bitcast_fusion) | data formatting | bytes 2097152 | tf_op jit(solution)/shard_map/reshape | solution.py:32
  80.3 1.0 reshape.159
  81.3 0.5 fusion.29
  81.8 1.1 copy.38
  82.8 11.8 %bitcast_convert_fusion.3 = (f32[2,64,128,128]{3,2,1,0:T(8,128)}, f32[2,64,128,128]{3,2,1,0:T(8,128)}) fusion(bf16[1,2,2,64,128,128]{5,4,3,2,1,0:T(8,128)(2,1)} %param.3), kind=kLoop, calls=%fused_computation.25 | loop fusion | flops 4194304 | bytes 25165824 | tf_op jit(solution)/shard_map/convert_element_type | solution.py:66
  94.6 8.8 %copy.31 = f32[2,64,128,128]{2,1,0,3:T(8,128)} copy(f32[2,64,128,128]{3,2,1,0:T(8,128)} %get-tuple-element.9) | data formatting | bytes 16777216 | tf_op jit(solution)/shard_map/convert_element_type | solution.py:66
  103.4 8.8 %copy.39 = f32[2,64,128,128]{2,1,0,3:T(8,128)} copy(f32[2,64,128,128]{3,2,1,0:T(8,128)} %get-tuple-element.10) | data formatting | bytes 16777216 | tf_op jit(solution)/shard_map/convert_element_type | solution.py:67
  112.7 95.5 %all-gather.2.cloned.1.call-done = bf16[2,128,4,64,128]{4,3,2,0,1:T(8,128)(2,1)} async-done(((bf16[2,8,4,64,128]{4,3,2,0,1:T(8,128)(2,1)}), bf16[2,128,4,64,128]{4,3,2,0,1:T(8,128)(2,1)}) %all-gather.2.cloned.1.call-update) | async-done | bytes 16777232 | tf_op jit(solution)/shard_map/all_gather | solution.py:62
  208.3 15.2 %fusion.58 = (bf16[1,4,64,128,128]{3,2,1,0,4:T(8,128)(2,1)}, bf16[1,4,64,128,128]{3,2,1,0,4:T(8,128)(2,1)}) fusion(bf16[2,4,64,128,128]{3,2,1,0,4:T(8,128)(2,1)} %bitcast.150), kind=kLoop, calls=%fused_computation.77 | loop fusion | bytes 33554432 | tf_op jit(solution)/shard_map/slice | solution.py:68
  223.5 17.5 %fusion.1 = (bf16[2,64,128,128]{2,1,0,3:T(8,128)(2,1)}, bf16[2,64,128,128]{2,1,0,3:T(8,128)(2,1)}) fusion(bf16[2,2,64,128,128]{3,2,1,0,4:T(8,128)(2,1)} %bitcast.148, bf16[2,2,64,128,128]{3,2,1,0,4:T(8,128)(2,1)} %bitcast.147, f32[2,64,128,128]{2,1,0,3:T(8,128)} %copy.39, f32[2,64,128,128]{2,1,0,3:T(8,128)S(1)} %copy-done), kind=kLoop, calls=%fused_computation.5 | loop fusion | flops 37748736 | bytes 41943040 | tf_op jit(solution)/shard_map/reduce_sum | solution.py:70
  240.9 7.0 %copy.89 = bf16[2,64,128,128]{2,3,1,0:T(8,128)(2,1)} copy(bf16[2,64,128,128]{2,1,0,3:T(8,128)(2,1)} %get-tuple-element.5) | data formatting | bytes 8388608 | tf_op jit(solution)/shard_map/reduce_sum | solution.py:70
  247.9 4.6 %copy.90 = bf16[2,64,128,128]{2,3,1,0:T(8,128)(2,1)} copy(bf16[2,64,128,128]{2,1,0,3:T(8,128)(2,1)S(1)} %copy-done.1) | data formatting | bytes 8388608 | tf_op jit(solution)/shard_map/reduce_sum | solution.py:71
  252.6 9.3 %fusion.7 = bf16[2,2,64,128,128]{4,3,0,2,1:T(8,128)(2,1)} fusion(bf16[1,2,64,128,128]{3,4,0,2,1:T(8,128)(2,1)} %bitcast.154, bf16[1,2,64,128,128]{3,4,0,2,1:T(8,128)(2,1)} %bitcast.153, bf16[1,2,128,128]{3,2,1,0:T(8,128)(2,1)S(1)} %get-tuple-element.18, bf16[1,2,128,128]{3,2,1,0:T(8,128)(2,1)S(1)} %get-tuple-element.17), kind=kOutput, calls=%fused_computation.12 | convolution fusion | flops 4320657408 | bytes 16908288 | tf_op jit(solution)/shard_map/pqkn,qrzxn->przxk/dot_general | solution.py:76
  261.9 12.2 %copy.43 = bf16[2,2,64,128,128]{4,0,2,1,3:T(2,128)(2,1)S(1)} copy(bf16[2,2,64,128,128]{4,3,0,2,1:T(8,128)(2,1)} %fusion.7) | data formatting | bytes 16777216 | tf_op jit(solution)/shard_map/convert_element_type | solution.py:78
  274.1 97.3 %all_to_all.43 = bf16[2,2,64,128,128]{4,0,2,1,3:T(2,128)(2,1)} all-to-all(bf16[2,2,64,128,128]{4,0,2,1,3:T(2,128)(2,1)S(1)} %copy.43), channel_id=1, replica_groups=mesh['grp'=16,'slab'=2] {'slab'}, dimensions={3} | all-to-all | bytes 16777216 | tf_op jit(solution)/shard_map/all_to_all | solution.py:82
  371.5 12.0 %copy.44 = bf16[2,2,64,128,128]{4,3,2,1,0:T(8,128)(2,1)} copy(bf16[2,2,64,128,128]{4,0,2,1,3:T(2,128)(2,1)} %all_to_all.43) | data formatting | bytes 16777216 | tf_op jit(solution)/shard_map/all_to_all | solution.py:82
  383.5 9.4 %copy.45 = bf16[2,2,2,64,64,128]{5,4,3,2,1,0:T(8,128)(2,1)} copy(bf16[2,2,2,64,64,128]{5,4,2,3,1,0:T(8,128)(2,1)} %bitcast.149) | data formatting | bytes 16777216 | tf_op jit(solution)/shard_map/all_to_all | solution.py:82
  392.8 21.3 %bitcast_reduce_fusion = bf16[64,128,128]{2,1,0:T(8,128)(2,1)S(1)} fusion(bf16[2,2,128,64,128]{4,3,2,1,0:T(8,128)(2,1)} %bitcast.152, bf16[1,128,128]{2,1,0:T(8,128)(2,1)S(1)} %get-tuple-element.22, bf16[1,128,128]{2,1,0:T(8,128)(2,1)S(1)} %fusion.51), kind=kOutput, calls=%fused_computation.17 | convolution fusion | flops 1074823168 | bytes 10551296 | tf_op jit(solution)/shard_map/qkn,qrnxy->rkxy/dot_general | solution.py:79
  414.2 2.8 copy.47
  (12 shorter events, 1.1 us)
Async XLA Ops:
  6.5 201.7 %all-gather.2.cloned.1.call-start = ((), (), s32[]{:S(2)}) async-start(), calls=%async_computation.3 | async-start | bytes 17825792 | tf_op jit(solution)/shard_map/all_gather | solution.py:62
  208.3 15.2 %copy-start = (f32[2,64,128,128]{2,1,0,3:T(8,128)S(1)}, f32[2,64,128,128]{2,1,0,3:T(8,128)}, u32[]{:S(2)}) copy-start(f32[2,64,128,128]{2,1,0,3:T(8,128)} %copy.31) | copy-start | bytes 25165828
  240.9 7.0 %copy-start.1 = (bf16[2,64,128,128]{2,1,0,3:T(8,128)(2,1)S(1)}, bf16[2,64,128,128]{2,1,0,3:T(8,128)(2,1)}, u32[]{:S(2)}) copy-start(bf16[2,64,128,128]{2,1,0,3:T(8,128)(2,1)} %get-tuple-element.6) | copy-start | bytes 12582916
Sparse Core Ops, SparseCore 0:
  83.0 125.2 all-gather.1
